TPU v7x, 512 devices: a whole 4x4x16 slice. The times are simulated.
512 devices in a mesh: rows: 128 (over x, z, core), cols: 4 (over y).
Axes of the slice: x: 4, y: 4, z: 16, core: 2. Of those that a mesh axis runs over, the one named last changes fastest.
Arguments:
- tiles: bfloat16 [65536, 4096], P(('rows', 'cols')), may hold values from -0.125 to 0.125
- integral_cd_tile: int32 [65536], P(('rows', 'cols')), may hold values from 0 to 511
- part_dest: int32 [16384, 1], P(('rows', 'cols')), may hold values from 0 to 127; in each aligned block of 32 rows (0 to 31, 32 to 63, ...) at most 2 rows name the same one
- partial_row_place: int32 [16384], P(('rows', 'cols')), may hold values from 0 to 15
- amplitudes: bfloat16 [4, 512, 4096], P('cols', 'rows'), may hold values from -6 to 6
- residual_in: float32 [128, 16, 4096], P('rows', 'cols'), may hold values from -6 to 6
Outputs:
- residual: float32 [128, 16, 4096], P('rows', 'cols')
Inputs may be any that keep to these rules, and one draw needn't show every extreme that they name: `part_dest`: among the 32 partial tiles of one device no index of rows is named more than 2 times, and at least one is named exactly 2 times.
All inputs are finite; a program needn't handle non-finite values.
Results may differ from a plain program's by a relative error of at most 0.0022.
Values may be sent and summed in bfloat16 or wider, within the bound.
A program may use at most 64 MiB of HBM per device.

v0:
```python
import jax
import jax.numpy as jnp
from jax import lax
from jax.sharding import PartitionSpec as P

TILE_SPAN = 64
NIJ = 64
TILES_PER_PART = 4
PAB = 32
OWNR = 16


def per_device(tiles, integral_cd_tile, part_dest, partial_row_place, amplitudes, residual_in):
    gathered = lax.all_gather(amplitudes, "rows", axis=1, tiled=True)[0]
    picked = jnp.take(gathered, integral_cd_tile, axis=0).reshape(
        PAB, TILES_PER_PART, NIJ, TILE_SPAN
    )
    block_list = tiles.reshape(PAB, TILES_PER_PART, TILE_SPAN, TILE_SPAN)
    per_tile = jnp.einsum("ptic,ptac->ptia", picked, block_list, preferred_element_type=jnp.float32)
    partial_value = jnp.sum(per_tile, axis=1)
    partial_value = partial_value.reshape(PAB, NIJ * TILE_SPAN).astype(jnp.bfloat16)
    row_count = lax.axis_size("rows")
    capacity = max(2, 2 * PAB // row_count)
    destination = part_dest[:, 0]
    onehot = (destination[:, None] == jnp.arange(row_count, dtype=jnp.int32)[None, :]).astype(
        jnp.int32
    )
    earlier = jnp.sum((jnp.cumsum(onehot, axis=0) - onehot) * onehot, axis=1)
    position = destination * capacity + earlier
    outgoing = (
        jnp.zeros((row_count * capacity, NIJ * TILE_SPAN), jnp.bfloat16)
        .at[position]
        .set(partial_value)
    )
    slot_ids = (
        jnp.full((row_count * capacity,), float(OWNR), jnp.float32)
        .at[position]
        .set(partial_row_place.astype(jnp.float32))
        .astype(jnp.bfloat16)
    )
    incoming, incoming_ids = (
        lax.all_to_all(
            outgoing.reshape(row_count, capacity, NIJ * TILE_SPAN),
            "rows",
            split_axis=0,
            concat_axis=0,
            tiled=True,
        ),
        lax.all_to_all(
            slot_ids.reshape(row_count, capacity), "rows", split_axis=0, concat_axis=0, tiled=True
        ),
    )
    incoming = incoming.reshape(row_count * capacity, NIJ * TILE_SPAN)
    incoming_ids = incoming_ids.reshape(row_count * capacity).astype(jnp.float32)
    select = (incoming_ids[None, :] == jnp.arange(OWNR, dtype=jnp.float32)[:, None]).astype(
        jnp.bfloat16
    )
    owned = jnp.dot(select, incoming, preferred_element_type=jnp.float32)
    shared = lax.psum_scatter(owned, "cols", scatter_dimension=0, tiled=True)
    return residual_in + shared[None, :, :]


def solution(mesh):
    return jax.shard_map(
        per_device,
        mesh=mesh,
        in_specs=(
            P(("rows", "cols"), None),
            P(("rows", "cols")),
            P(("rows", "cols"), None),
            P(("rows", "cols")),
            P("cols", "rows", None),
            P("rows", "cols", None),
        ),
        out_specs=P("rows", "cols", None),
        check_vma=False,
    )
```

profile of v0, /device:TPU:2, one launch (start us, length us, event | category | flops | bytes accessed | tf_op | source)
XLA Modules:
  0.0 361.6 jit_solution(1006233409174559257)
XLA Ops:
  6.5 0.0 copy-start.1
  6.5 0.0 all-gather.2.cloned.1.call-start
  6.5 1.4 copy.10
  8.0 0.0 all-gather.2.cloned.1.call-update
  8.0 0.7 convert_element_type.27
  8.7 0.7 fusion.13
  9.4 0.1 reduce_window_sum.11
  9.5 0.8 select_reduce_fusion
  10.3 0.7 fusion.16
  11.0 0.7 scatter_custom_fusion
  11.6 0.8 all_to_all.12
  12.4 19.5 %all-to-all-start = ((bf16[128,1,2]{2,1,0:T(2,128)(2,1)}), bf16[128,1,2]{2,1,0:T(2,128)(2,1)S(1)}, u32[]{:S(2)}, u32[]{:S(2)}) async-start(bf16[128,1,2]{2,1,0:T(2,128)(2,1)} %all_to_all.12), calls=%async_computation | async-start | bytes 131072 | tf_op jit(solution)/shard_map/all_to_all | solution.py:49
  32.0 3.3 reshape.37
  35.2 0.0 copy-done.1
  35.3 0.1 broadcast_in_dim.30
  35.4 125.5 %all-gather.2.cloned.1.call-done = bf16[1,512,4096]{2,0,1:T(2,128)(2,1)} async-done(((bf16[1,4,4096]{2,0,1:T(2,128)(2,1)}), bf16[1,512,4096]{2,0,1:T(2,128)(2,1)}) %all-gather.2.cloned.1.call-update) | async-done | bytes 4194320 | tf_op jit(solution)/shard_map/all_gather | solution.py:14
  160.9 10.1 %copy.14 = bf16[1,512,4096]{2,1,0:T(8,128)(2,1)} copy(bf16[1,512,4096]{2,0,1:T(2,128)(2,1)} %all-gather.2.cloned.1.call-done) | data formatting | bytes 8388608
  171.0 4.9 %gather_fusion = bf16[128,4096]{1,0:T(8,128)(2,1)S(1)} fusion(bf16[512,4096]{1,0:T(8,128)(2,1)} %bitcast.22, s32[1024]{0:T(1024)S(1)} %pad_clamp_fusion), kind=kCustom, calls=%fused_computation | custom fusion | bytes 2097664 | tf_op jit(solution)/shard_map/jit(_take)/gather | solution.py:15
  175.9 3.3 gather.7
  179.2 2.4 fusion.6
  181.6 0.5 reshape.61
  182.0 2.0 scatter_custom_fusion.1
  184.0 2.7 reshape.38
  186.7 0.0 all-to-all-done
  186.7 11.6 %all-to-all-start.1 = ((bf16[128,2,4096]{2,1,0:T(2,128)(2,1)}), bf16[128,2,4096]{2,1,0:T(2,128)(2,1)S(1)}, u32[]{:S(2)}, u32[]{:S(2)}) async-start(bf16[128,2,4096]{2,1,0:T(2,128)(2,1)} %reshape.38), calls=%async_computation.1 | async-start | bytes 4194304 | tf_op jit(solution)/shard_map/all_to_all | solution.py:42
  198.3 0.0 all-reduce.3.cloned.1.call-start
  198.4 0.2 convert_reduce_fusion
  198.6 0.1 reshape.40
  198.7 98.9 %all-to-all-done.1 = bf16[128,2,4096]{2,1,0:T(2,128)(2,1)S(1)} async-done(((bf16[128,2,4096]{2,1,0:T(2,128)(2,1)}), bf16[128,2,4096]{2,1,0:T(2,128)(2,1)S(1)}, u32[]{:S(2)}, u32[]{:S(2)}) %all-to-all-start.1) | async-done | bytes 2097184 | tf_op jit(solution)/shard_map/all_to_all | solution.py:42
  297.6 2.2 reshape.39
  299.8 0.0 copy-start
  299.9 2.7 fusion.14
  302.6 0.0 all-reduce.3.cloned.1.call-update
  302.6 1.3 dynamic-slice
  304.5 48.7 %all-reduce.3.cloned.1.call-done = f32[16,4096]{1,0:T(8,128)} async-done(((f32[16,4096]{1,0:T(8,128)}), f32[16,4096]{1,0:T(8,128)}) %all-reduce.3.cloned.1.call-update) | async-done | bytes 262160
  353.2 0.0 copy-done
  353.2 1.6 fusion.12
  (4 shorter events, 0.0 us)
Async XLA Ops:
  6.5 28.7 %copy-start.1 = (s32[128]{0:T(128)S(1)}, s32[128]{0:T(128)}, u32[]{:S(2)}) copy-start(s32[128]{0:T(128)} %param.7) | copy-start | bytes 1540
  6.5 154.3 %all-gather.2.cloned.1.call-start = ((), (), s32[]{:S(2)}) async-start(), calls=%async_computation.2 | async-start | bytes 8454144 | tf_op jit(solution)/shard_map/all_gather | solution.py:14
  12.4 174.3 %all-to-all-start = ((bf16[128,1,2]{2,1,0:T(2,128)(2,1)}), bf16[128,1,2]{2,1,0:T(2,128)(2,1)S(1)}, u32[]{:S(2)}, u32[]{:S(2)}) async-start(bf16[128,1,2]{2,1,0:T(2,128)(2,1)} %all_to_all.12), calls=%async_computation | async-start | bytes 131072 | tf_op jit(solution)/shard_map/all_to_all | solution.py:49
  186.7 110.9 %all-to-all-start.1 = ((bf16[128,2,4096]{2,1,0:T(2,128)(2,1)}), bf16[128,2,4096]{2,1,0:T(2,128)(2,1)S(1)}, u32[]{:S(2)}, u32[]{:S(2)}) async-start(bf16[128,2,4096]{2,1,0:T(2,128)(2,1)} %reshape.38), calls=%async_computation.1 | async-start | bytes 4194304 | tf_op jit(solution)/shard_map/all_to_all | solution.py:42
  198.3 154.9 %all-reduce.3.cloned.1.call-start = ((), (), s32[]{:S(2)}) async-start(), calls=%async_computation.3 | async-start | bytes 524288
  299.8 53.4 %copy-start = (f32[1,4,4096]{2,1,0:T(4,128)S(1)}, f32[1,4,4096]{2,1,0:T(4,128)}, u32[]{:S(2)}) copy-start(f32[1,4,4096]{2,1,0:T(4,128)} %param.11) | copy-start | bytes 196612
Sparse Core Ops, SparseCore 0:
  10.5 150.3 all-gather.1
  302.7 50.4 all-reduce.2
where the time goes:
time: 362 us
  waiting for transfers between devices  273 us (75%)
  local copies, waits for them, and re-layouts  33.4 us (9%)
  starting transfers between devices  31.2 us (9%)
  between operations  14.2 us (4%)
  matrix products  5.09 us (1%)
  other arithmetic  4.7 us (1%)
    all_gather x1, waiting for transfers between devices, per_device(): gathered = lax.all_gather(amplitudes, 'rows', axis=1, tiled=True)[0]  125 us
    all_to_all x1, waiting for transfers between devices, per_device(): lax.all_to_all(outgoing.reshape(row_count, capacity, NIJ * TILE_SPAN), 'r...  98.9 us
    unnamed x3, waiting for transfers between devices  48.7 us
    all_to_all x1, starting transfers between devices, per_device(): lax.all_to_all(slot_ids.reshape(row_count, capacity), 'rows', split_axis=...  19.5 us
    unnamed x7, local copies, waits for them, and re-layouts  12.8 us
    all_to_all x1, starting transfers between devices, per_device(): lax.all_to_all(outgoing.reshape(row_count, capacity, NIJ * TILE_SPAN), 'r...  11.6 us
    gather x2, local copies, waits for them, and re-layouts, per_device(): jnp.take(gathered, integral_cd_tile, axis=0)  8.25 us
  transfers between devices with their start and end apart: 4, of which 3 were waited for; matrix products, arithmetic and copies ran while one was open for 10% of the time, Pallas kernels for 0%

commit v1 on v0

--- a/solution.py
+++ b/solution.py
@@ -11,7 +11,9 @@
 
 
 def per_device(tiles, integral_cd_tile, part_dest, partial_row_place, amplitudes, residual_in):
-    gathered = lax.all_gather(amplitudes, "rows", axis=1, tiled=True)[0]
+    gathered = jnp.concatenate(
+        lax.all_to_all(jnp.stack([amplitudes] * lax.axis_size("rows")), "rows", 0, 0), axis=1
+    )[0]
     picked = jnp.take(gathered, integral_cd_tile, axis=0).reshape(
         PAB, TILES_PER_PART, NIJ, TILE_SPAN
     )

time: 362 us -> 432 us (1.19)
  waiting for transfers between devices: 273 us -> 331 us
  starting transfers between devices: 31.2 us -> 46.2 us
    all_to_all x0 -> x1, waiting for transfers between devices: none -> 183 us  [per_device(): lax.all_to_all(jnp.stack([amplitudes] * lax.axis_size('rows')), 'rows', 0...]
    all_gather x1 -> x0, waiting for transfers between devices: 125 us -> none  [per_device(): gathered = lax.all_gather(amplitudes, 'rows', axis=1, tiled=True)[0]]
    all_to_all x0 -> x1, starting transfers between devices: none -> 20.1 us  [per_device(): lax.all_to_all(jnp.stack([amplitudes] * lax.axis_size('rows')), 'rows', 0...]
    another operation x0 -> x2, local copies, waits for them, and re-layouts: none -> 11.7 us  [the longest x1 6.91 us: per_device(): jnp.concatenate(lax.all_to_all(jnp.stack([amplitudes] * lax.axis_size('ro...]
    unnamed x7 -> x11, local copies, waits for them, and re-layouts: 12.8 us -> 1.3 us
    all_to_all x1, starting transfers between devices: 19.5 us -> 9.86 us  [per_device(): lax.all_to_all(slot_ids.reshape(row_count, capacity), 'rows', split_axis=...]
    all_to_all x1, starting transfers between devices: 11.6 us -> 16.2 us  [per_device(): lax.all_to_all(outgoing.reshape(row_count, capacity, NIJ * TILE_SPAN), 'r...]
    unnamed x3 -> x2, waiting for transfers between devices: 48.7 us -> 48.9 us
  transfers between devices with their start and end apart: 4 -> 4, of which waited for: 3 -> 3; matrix products, arithmetic and copies ran while one was open for 10% -> 6% of each run, Pallas kernels for 0% -> 0%
where the time goes in v1:
time: 432 us; the launch traced here: 431 us
  waiting for transfers between devices  331 us (77%)
  starting transfers between devices  46.2 us (11%)
  local copies, waits for them, and re-layouts  32.6 us (8%)
  between operations  14.2 us (3%)
  matrix products  5.08 us (1%)
    all_to_all x1, waiting for transfers between devices, per_device(): lax.all_to_all(jnp.stack([amplitudes] * lax.axis_size('rows')), 'rows', 0...  183 us
    all_to_all x1, waiting for transfers between devices, per_device(): lax.all_to_all(outgoing.reshape(row_count, capacity, NIJ * TILE_SPAN), 'r...  98.9 us
    unnamed x2, waiting for transfers between devices  48.9 us
    all_to_all x1, starting transfers between devices, per_device(): lax.all_to_all(jnp.stack([amplitudes] * lax.axis_size('rows')), 'rows', 0...  20.1 us
    all_to_all x1, starting transfers between devices, per_device(): lax.all_to_all(outgoing.reshape(row_count, capacity, NIJ * TILE_SPAN), 'r...  16.2 us
    all_to_all x1, starting transfers between devices, per_device(): lax.all_to_all(slot_ids.reshape(row_count, capacity), 'rows', split_axis=...  9.86 us
  transfers between devices with their start and end apart: 4, of which 3 were waited for; matrix products, arithmetic and copies ran while one was open for 6% of the time, Pallas kernels for 0%

profile of v1, /device:TPU:2, one launch (start us, length us, event | category | flops | bytes accessed | tf_op | source)
XLA Modules:
  0.0 431.1 jit_solution(15949488717807850824)
XLA Ops:
  6.5 4.8 %stack.2 = bf16[128,1,4,4096]{3,2,1,0:T(4,128)(2,1)} broadcast(bf16[4,4096]{1,0:T(4,128)(2,1)} %bitcast.20), dimensions={2,3} | broadcast | bytes 4227072 | tf_op jit(solution)/shard_map/stack | solution.py:15
  11.4 0.0 copy-start
  11.4 20.1 %all-to-all-start.1 = ((bf16[128,1,4,4096]{3,2,1,0:T(4,128)(2,1)}), bf16[128,1,4,4096]{3,2,1,0:T(4,128)(2,1)}, u32[]{:S(2)}, u32[]{:S(2)}) async-start(bf16[128,1,4,4096]{3,2,1,0:T(4,128)(2,1)} %stack.2), calls=%async_computation.1 | async-start | bytes 8388608 | tf_op jit(solution)/shard_map/all_to_all | solution.py:15
  31.5 0.0 copy-done
  31.5 0.0 copy-start.4
  31.5 0.0 copy-start.3
  31.5 0.0 copy-start.2
  31.5 2.3 reshape.40
  33.8 0.0 copy-done.4
  33.8 0.1 broadcast_in_dim.30
  34.0 0.0 copy-done.3
  34.0 0.0 copy-done.2
  34.0 0.1 fusion.13
  34.1 0.1 reduce_window_sum.11
  34.1 0.2 select_reduce_fusion
  34.3 0.7 scatter_custom_fusion
  35.0 0.8 all_to_all.16
  35.8 183.2 %all-to-all-done.1 = bf16[128,1,4,4096]{3,2,1,0:T(4,128)(2,1)} async-done(((bf16[128,1,4,4096]{3,2,1,0:T(4,128)(2,1)}), bf16[128,1,4,4096]{3,2,1,0:T(4,128)(2,1)}, u32[]{:S(2)}, u32[]{:S(2)}) %all-to-all-start.1) | async-done | bytes 4194336 | tf_op jit(solution)/shard_map/all_to_all | solution.py:15
  219.0 9.9 %all-to-all-start = ((bf16[128,1,2]{2,1,0:T(2,128)(2,1)}), bf16[128,1,2]{2,1,0:T(2,128)(2,1)S(1)}, u32[]{:S(2)}, u32[]{:S(2)}) async-start(bf16[128,1,2]{2,1,0:T(2,128)(2,1)} %all_to_all.16), calls=%async_computation | async-start | bytes 131072 | tf_op jit(solution)/shard_map/all_to_all | solution.py:51
  228.9 6.9 %squeeze_reshape.3 = bf16[512,4096]{1,0:T(8,128)(2,1)} reshape(bf16[128,1,4,4096]{3,2,1,0:T(4,128)(2,1)} %all-to-all-done.1) | data formatting | bytes 8388608 | tf_op jit(solution)/shard_map/squeeze;reshape | solution.py:14
  235.8 4.9 %gather_fusion = bf16[128,4096]{1,0:T(8,128)(2,1)S(1)} fusion(bf16[512,4096]{1,0:T(8,128)(2,1)} %squeeze_reshape.3, s32[1024]{0:T(1024)S(1)} %pad_clamp_fusion), kind=kCustom, calls=%fused_computation | custom fusion | bytes 2097664 | tf_op jit(solution)/shard_map/jit(_take)/gather | solution.py:17
  240.7 3.3 gather.7
  244.0 2.3 fusion.6
  246.4 0.5 reshape.64
  246.9 2.0 scatter_custom_fusion.1
  248.8 2.7 reshape.41
  251.5 0.0 all-to-all-done
  251.5 16.2 %all-to-all-start.2 = ((bf16[128,2,4096]{2,1,0:T(2,128)(2,1)}), bf16[128,2,4096]{2,1,0:T(2,128)(2,1)S(1)}, u32[]{:S(2)}, u32[]{:S(2)}) async-start(bf16[128,2,4096]{2,1,0:T(2,128)(2,1)} %reshape.41), calls=%async_computation.2 | async-start | bytes 4194304 | tf_op jit(solution)/shard_map/all_to_all | solution.py:44
  267.7 0.0 all-reduce.3.cloned.1.call-start
  267.7 0.2 convert_reduce_fusion
  267.9 0.1 reshape.43
  268.1 98.9 %all-to-all-done.2 = bf16[128,2,4096]{2,1,0:T(2,128)(2,1)S(1)} async-done(((bf16[128,2,4096]{2,1,0:T(2,128)(2,1)}), bf16[128,2,4096]{2,1,0:T(2,128)(2,1)S(1)}, u32[]{:S(2)}, u32[]{:S(2)}) %all-to-all-start.2) | async-done | bytes 2097184 | tf_op jit(solution)/shard_map/all_to_all | solution.py:44
  367.0 2.2 reshape.42
  369.2 0.0 copy-start.1
  369.2 2.7 fusion.14
  371.9 0.0 all-reduce.3.cloned.1.call-update
  371.9 1.3 dynamic-slice
  373.9 48.9 %all-reduce.3.cloned.1.call-done = f32[16,4096]{1,0:T(8,128)} async-done(((f32[16,4096]{1,0:T(8,128)}), f32[16,4096]{1,0:T(8,128)}) %all-reduce.3.cloned.1.call-update) | async-done | bytes 262160
  422.7 0.0 copy-done.1
  422.7 1.6 fusion.12
  (6 shorter events, 0.0 us)
Async XLA Ops:
  11.4 20.1 %copy-start = (bf16[128,4096]{1,0:T(8,128)(2,1)S(1)}, bf16[128,4096]{1,0:T(8,128)(2,1)}, u32[]{:S(2)}) copy-start(bf16[128,4096]{1,0:T(8,128)(2,1)} %param.6) | copy-start | bytes 3145732
  11.4 207.7 %all-to-all-start.1 = ((bf16[128,1,4,4096]{3,2,1,0:T(4,128)(2,1)}), bf16[128,1,4,4096]{3,2,1,0:T(4,128)(2,1)}, u32[]{:S(2)}, u32[]{:S(2)}) async-start(bf16[128,1,4,4096]{3,2,1,0:T(4,128)(2,1)} %stack.2), calls=%async_computation.1 | async-start | bytes 8388608 | tf_op jit(solution)/shard_map/all_to_all | solution.py:15
  31.5 2.3 copy-start.4
  31.5 2.5 copy-start.3
  31.5 2.5 copy-start.2
  219.0 32.5 %all-to-all-start = ((bf16[128,1,2]{2,1,0:T(2,128)(2,1)}), bf16[128,1,2]{2,1,0:T(2,128)(2,1)S(1)}, u32[]{:S(2)}, u32[]{:S(2)}) async-start(bf16[128,1,2]{2,1,0:T(2,128)(2,1)} %all_to_all.16), calls=%async_computation | async-start | bytes 131072 | tf_op jit(solution)/shard_map/all_to_all | solution.py:51
  251.5 115.5 %all-to-all-start.2 = ((bf16[128,2,4096]{2,1,0:T(2,128)(2,1)}), bf16[128,2,4096]{2,1,0:T(2,128)(2,1)S(1)}, u32[]{:S(2)}, u32[]{:S(2)}) async-start(bf16[128,2,4096]{2,1,0:T(2,128)(2,1)} %reshape.41), calls=%async_computation.2 | async-start | bytes 4194304 | tf_op jit(solution)/shard_map/all_to_all | solution.py:44
  267.7 155.0 %all-reduce.3.cloned.1.call-start = ((), (), s32[]{:S(2)}) async-start(), calls=%async_computation.3 | async-start | bytes 524288
  369.2 53.5 %copy-start.1 = (f32[1,4,4096]{2,1,0:T(4,128)S(1)}, f32[1,4,4096]{2,1,0:T(4,128)}, u32[]{:S(2)}) copy-start(f32[1,4,4096]{2,1,0:T(4,128)} %param.11) | copy-start | bytes 196612
Sparse Core Ops, SparseCore 0:
  372.1 50.6 all-reduce.2
